TPU v7x, 256 devices: a whole 4x4x8 slice. The times are simulated.
256 devices in a mesh: batch: 4 (over x_hi, core), hidden: 16 (over x_lo, z), width: 4 (over y).
Axes of the slice: x: 4 (x_hi: 2, x_lo: 2; x = x_hi * 2 + x_lo), y: 4, z: 8, core: 2. Of those that a mesh axis runs over, the one named last changes fastest.
Arguments:
- frames: bfloat16 [4, 512, 1280], P('batch', None, 'hidden'), may hold values from -6 to 6
- adapter_weight: bfloat16 [4, 1280, 16384], P(None, 'hidden', 'width'), may hold values from -0.078125 to 0.078125
- text_embed: bfloat16 [512, 16384], P('batch', 'width'), may hold values from -6 to 6
- audio_len: int32 [4], P('batch'), may hold values from 16 to 64, as said below
- text_len: int32 [4], P('batch'), may hold values from 32 to 112, as said below
- norm_gain: bfloat16 [16384], P('width'), may hold values from 0.5 to 1.5
- gate_up: bfloat16 [16384, 2, 26624], P('width', None, ('batch', 'hidden')), may hold values from -0.046875 to 0.046875
- cotangent: bfloat16 [512, 26624], P('width', ('batch', 'hidden')), may hold values from -0.59765625 to 0.59765625
Outputs:
- hidden: bfloat16 [512, 26624], P('width', ('batch', 'hidden'))
- weight_grad: float32 [4, 1280, 16384], P(None, 'hidden', 'width')
Inputs may be any that keep to these rules, and one draw needn't show every extreme that they name: `audio_len`: some sequence holds exactly 16 audio positions and another exactly 64. audio_len + text_len never exceeds 128, and equals it in some sequence.
All inputs are finite; a program needn't handle non-finite values.
Results may differ from a plain program's by a relative error of at most 0.0059.
Values may be sent and summed in bfloat16 or wider, within the bound.
A program may use at most 64 MiB of HBM per device.

v0:
```python
import jax
import jax.numpy as jnp
from jax import lax
from jax.sharding import PartitionSpec as P

D = 16384
norm_eps = 1e-05


def row_lookup(table, row_index):
    slots = jnp.arange(table.shape[0], dtype=jnp.int32)
    return jnp.sum(jnp.where(row_index[:, None] == slots[None, :], table[None, :], 0), axis=1)


def on_device(
    frames, adapter_weight, text_embed, audio_len, text_len, norm_gain, gate_up, cotangent
):
    rows_here, frame_count, feat_here = frames.shape
    seq_len = frame_count // 4
    width_here = adapter_weight.shape[2]
    tok_here = rows_here * seq_len
    stacked = frames.reshape(tok_here, 4 * feat_here)
    kernel = adapter_weight.reshape(4 * feat_here, width_here)
    partial_audio = jnp.dot(stacked, kernel, preferred_element_type=jnp.float32)
    audio_part = lax.psum(partial_audio, "hidden")
    local_index = jnp.arange(tok_here, dtype=jnp.int32)
    row_index = local_index // seq_len
    positions = local_index % seq_len
    audio_count = row_lookup(audio_len, row_index)
    text_count = row_lookup(text_len, row_index)
    is_audio = positions < audio_count
    is_text = jnp.logical_and(jnp.logical_not(is_audio), positions < audio_count + text_count)
    stream = jnp.where(
        is_audio[:, None],
        audio_part,
        jnp.where(is_text[:, None], text_embed.astype(jnp.float32), jnp.zeros_like(audio_part)),
    )
    sum_squares = lax.psum(jnp.sum(stream * stream, axis=1), "width")
    inv_rms = lax.rsqrt(sum_squares / D + norm_eps)
    unit_stream = stream * inv_rms[:, None]
    gain_vals = norm_gain.astype(jnp.float32)
    normed = (unit_stream * gain_vals[None, :]).astype(jnp.bfloat16)
    weights = gate_up.reshape(width_here, -1)
    half_cols = weights.shape[1] // 2
    partial_pair = jnp.dot(
        lax.all_gather(normed, "batch", axis=0, tiled=True),
        weights,
        preferred_element_type=jnp.float32,
    )
    summed = lax.psum_scatter(partial_pair, "width", scatter_dimension=0, tiled=True)
    gate_vals = summed[:, :half_cols]
    up_vals = summed[:, half_cols:]
    sigmoid_gate = jax.nn.sigmoid(gate_vals)
    silu_gate = gate_vals * sigmoid_gate
    hidden = (silu_gate * up_vals).astype(jnp.bfloat16)
    cot_vals = cotangent.astype(jnp.float32)
    silu_slope = sigmoid_gate * (1.0 + gate_vals * (1.0 - sigmoid_gate))
    grad_pair = jnp.concatenate(
        [
            (cot_vals * up_vals * silu_slope).astype(jnp.bfloat16),
            (cot_vals * silu_gate).astype(jnp.bfloat16),
        ],
        axis=1,
    )
    all_pairs = lax.all_gather(grad_pair, "width", axis=0, tiled=True)
    share_rows = tok_here // lax.axis_size("hidden")
    row_block = all_pairs
    normed_grad = lax.psum_scatter(
        lax.dot_general(
            row_block, weights, (((1,), (1,)), ((), ())), preferred_element_type=jnp.float32
        ),
        ("batch", "hidden"),
        scatter_dimension=0,
        tiled=True,
    )
    share_start = lax.axis_index("hidden") * share_rows
    unit_share = lax.dynamic_slice_in_dim(unit_stream, share_start, share_rows, 0)
    inv_share = lax.dynamic_slice_in_dim(inv_rms, share_start, share_rows, 0)
    audio_share = lax.dynamic_slice_in_dim(is_audio, share_start, share_rows, 0)
    scaled_grad = normed_grad * gain_vals[None, :]
    proj_stat = lax.psum(jnp.sum(unit_share * scaled_grad, axis=1), "width") / D
    stream_grad = (scaled_grad - unit_share * proj_stat[:, None]) * inv_share[:, None]
    audio_grad = jnp.where(audio_share[:, None], stream_grad, jnp.zeros_like(stream_grad)).astype(
        jnp.bfloat16
    )
    row_block = stacked
    local_grad = lax.dot_general(
        row_block,
        lax.all_gather(audio_grad, "hidden", axis=0, tiled=True),
        (((0,), (0,)), ((), ())),
        preferred_element_type=jnp.float32,
    )
    weight_grad = lax.psum(local_grad, "batch")
    return (hidden, weight_grad.reshape(4, feat_here, width_here))


def solution(mesh):
    return jax.shard_map(
        on_device,
        mesh=mesh,
        in_specs=(
            P("batch", None, "hidden"),
            P(None, "hidden", "width"),
            P("batch", "width"),
            P("batch"),
            P("batch"),
            P("width"),
            P("width", None, ("batch", "hidden")),
            P("width", ("batch", "hidden")),
        ),
        out_specs=(P("width", ("batch", "hidden")), P(None, "hidden", "width")),
        check_vma=False,
    )
```

profile of v0, /device:TPU:1, one launch (start us, length us, event | category | flops | bytes accessed | tf_op | source)
XLA Modules:
  0.0 757.5 jit_solution(508925325179178368)
XLA Ops:
  7.2 1.2 copy.10
  8.4 0.1 reshape.64
  8.5 0.4 copy-done
  8.9 2.0 fusion.8
  11.1 0.6 copy-done.2
  13.0 134.5 %all-reduce.3.cloned.1.call-done = f32[128,4096]{1,0:T(8,128)} async-done(((f32[128,4096]{1,0:T(8,128)}), f32[128,4096]{1,0:T(8,128)}) %all-reduce.3.cloned.1.call-update) | async-done | bytes 2097168 | tf_op jit(solution)/shard_map/psum | solution.py:25
  147.4 2.4 multiply_reduce_fusion
  149.8 8.7 %psum.29 = f32[128]{0:T(128)S(1)} all-reduce(f32[128]{0:T(128)S(1)} %multiply_reduce_fusion), channel_id=1, replica_groups=mesh['batch'=4,'hidden'=16,'width'=4] {'width'}, use_global_device_ids=true, to_apply=%region_2.3 | all-reduce | flops 128 | bytes 1024 | tf_op jit(solution)/shard_map/psum | solution.py:38
  158.5 4.1 multiply_convert_fusion
  162.7 48.2 %all-gather.3.cloned.1.call-done = bf16[512,4096]{1,0:T(8,128)(2,1)} async-done(((bf16[128,4096]{1,0:T(8,128)(2,1)}), bf16[512,4096]{1,0:T(8,128)(2,1)}) %all-gather.3.cloned.1.call-update) | async-done | bytes 4194320 | tf_op jit(solution)/shard_map/all_gather | solution.py:46
  210.9 9.2 %fusion.9 = f32[512,832]{0,1:T(8,128)} fusion(bf16[512,4096]{1,0:T(8,128)(2,1)} %all-gather.3.cloned.1.call-done, bf16[4096,832]{0,1:T(8,128)(2,1)} %bitcast.19), kind=kOutput, calls=%fused_computation.28 | convolution fusion | flops 3489660928 | bytes 12713984 | tf_op jit(solution)/shard_map/dot_general | solution.py:45
  220.1 28.2 %reduce-scatter.3.cloned.1.call-done = f32[128,832]{0,1:T(8,128)} async-done(((f32[512,832]{0,1:T(8,128)}), f32[128,832]{0,1:T(8,128)}) %reduce-scatter.3.cloned.1.call-update) | async-done | bytes 426000 | tf_op jit(solution)/shard_map/reduce_scatter | solution.py:50
  248.3 1.8 fusion.2
  250.1 17.1 %all_gather.10 = bf16[512,832]{0,1:T(8,128)(2,1)S(1)} all-gather(bf16[128,832]{0,1:T(8,128)(2,1)S(1)} %pad_maximum_fusion), channel_id=1, replica_groups=mesh['batch'=4,'hidden'=16,'width'=4] {'width'}, dimensions={0}, use_global_device_ids=true | all-gather | bytes 1064960 | tf_op jit(solution)/shard_map/all_gather | solution.py:65
  267.2 9.7 %fusion.10 = f32[512,4096]{1,0:T(8,128)} fusion(bf16[512,832]{0,1:T(8,128)(2,1)S(1)} %all_gather.10, bf16[4096,832]{0,1:T(8,128)(2,1)} %bitcast.20), kind=kOutput, calls=%fused_computation.29 | convolution fusion | flops 3489660928 | bytes 16056320 | tf_op jit(solution)/shard_map/dot_general | solution.py:69
  277.0 0.1 dynamic_slice.9
  277.0 260.5 %reduce-scatter.5.cloned.1.call-done = f32[8,4096]{1,0:T(8,128)} async-done(((f32[512,4096]{1,0:T(8,128)}), f32[8,4096]{1,0:T(8,128)}) %reduce-scatter.5.cloned.1.call-update) | async-done | bytes 131088 | tf_op jit(solution)/shard_map/reduce_scatter | solution.py:68
  537.6 1.1 multiply_reduce_fusion.1
  538.8 8.8 %psum.30 = f32[8]{0:T(128)S(1)} all-reduce(f32[8]{0:T(128)S(1)} %multiply_reduce_fusion.1), channel_id=1, replica_groups=mesh['batch'=4,'hidden'=16,'width'=4] {'width'}, use_global_device_ids=true, to_apply=%region_6.7 | all-reduce | flops 8 | bytes 64 | tf_op jit(solution)/shard_map/psum | solution.py:81
  547.6 1.7 select_convert_fusion
  549.4 67.9 %all-gather.5.cloned.1.call-done = bf16[128,4096]{1,0:T(8,128)(2,1)} async-done(((bf16[8,4096]{1,0:T(8,128)(2,1)}), bf16[128,4096]{1,0:T(8,128)(2,1)}) %all-gather.5.cloned.1.call-update) | async-done | bytes 1048592 | tf_op jit(solution)/shard_map/all_gather | solution.py:89
  617.3 4.5 fusion.11
  621.8 123.5 %all-reduce.5.cloned.1.call-done = f32[4,80,4096]{2,1,0:T(8,128)} async-done(((f32[4,80,4096]{2,1,0:T(8,128)}), f32[4,80,4096]{2,1,0:T(8,128)}) %all-reduce.5.cloned.1.call-update) | async-done | bytes 5242896 | tf_op jit(solution)/shard_map/psum | solution.py:93
  745.2 5.4 copy.15
  (22 shorter events, 0.5 us)
Async XLA Ops:
  7.2 1.8 copy-start
  7.2 140.3 %all-reduce.3.cloned.1.call-start = ((), (), s32[]{:S(2)}) async-start(), calls=%async_computation.2 | async-start | bytes 4194304 | tf_op jit(solution)/shard_map/psum | solution.py:25
  11.0 0.7 copy-start.2
  11.0 199.9 %all-gather.3.cloned.1.call-start = ((), (), s32[]{:S(2)}) async-start(), calls=%async_computation.3 | async-start | bytes 5242880 | tf_op jit(solution)/shard_map/all_gather | solution.py:46
  162.6 85.7 %reduce-scatter.3.cloned.1.call-start = ((), (), s32[]{:S(2)}) async-start(), calls=%async_computation.4 | async-start | bytes 2129920 | tf_op jit(solution)/shard_map/reduce_scatter | solution.py:50
  210.9 37.4 %copy-start.1 = (bf16[128,416]{0,1:T(8,128)(2,1)S(1)}, bf16[128,416]{0,1:T(8,128)(2,1)}, u32[]{:S(2)}) copy-start(bf16[128,416]{0,1:T(8,128)(2,1)} %param.15) | copy-start | bytes 319492
  220.1 317.5 %reduce-scatter.5.cloned.1.call-start = ((), (), s32[]{:S(2)}) async-start(), calls=%async_computation.5 | async-start | bytes 8519680 | tf_op jit(solution)/shard_map/reduce_scatter | solution.py:68
  276.9 340.4 %all-gather.5.cloned.1.call-start = ((), (), s32[]{:S(2)}) async-start(), calls=%async_computation.6 | async-start | bytes 1114112 | tf_op jit(solution)/shard_map/all_gather | solution.py:89
  549.3 195.9 %all-reduce.5.cloned.1.call-start = ((), (), s32[]{:S(2)}) async-start(), calls=%async_computation.7 | async-start | bytes 10485760 | tf_op jit(solution)/shard_map/psum | solution.py:93
Sparse Core Ops, SparseCore 0:
  11.2 136.1 all-reduce.2
  162.8 48.0 all-gather.2
  220.2 28.0 reduce-scatter.2
  277.0 260.5 reduce-scatter.4
  549.4 67.7 all-gather.4
  621.9 123.2 all-reduce.4
where the time goes:
time: 758 us
  waiting for transfers between devices  663 us (87%)
  blocking collectives  34.6 us (5%)
  matrix products  25.3 us (3%)
  between operations  15.5 us (2%)
  other arithmetic  11.1 us (1%)
  local copies, waits for them, and re-layouts  7.94 us (1%)
    reduce_scatter x1, waiting for transfers between devices, on_device(): lax.psum_scatter(lax.dot_general(row_block, weights, (((1,), (1,)), ((),...  261 us
    psum x1, waiting for transfers between devices, on_device(): audio_part = lax.psum(partial_audio, 'hidden')  134 us
    psum x1, waiting for transfers between devices, on_device(): weight_grad = lax.psum(local_grad, 'batch')  123 us
    all_gather x1, waiting for transfers between devices, on_device(): lax.all_gather(audio_grad, 'hidden', axis=0, tiled=True)  67.9 us
    all_gather x1, waiting for transfers between devices, on_device(): lax.all_gather(normed, 'batch', axis=0, tiled=True)  48.2 us
    reduce_scatter x1, waiting for transfers between devices, on_device(): lax.psum_scatter(partial_pair, 'width', scatter_dimension=0, tiled=True)  28.2 us
    all_gather x1, blocking collectives, on_device(): all_pairs = lax.all_gather(grad_pair, 'width', axis=0, tiled=True)  17.1 us
  transfers between devices with their start and end apart: 6, of which 6 were waited for; matrix products, arithmetic and copies ran while one was open for 0% of the time, Pallas kernels for 0%

commit v1 on v0

--- a/solution.py
+++ b/solution.py
@@ -90,7 +90,7 @@
         (((0,), (0,)), ((), ())),
         preferred_element_type=jnp.float32,
     )
-    weight_grad = lax.psum(local_grad, "batch")
+    weight_grad = jnp.sum(lax.all_gather(local_grad, "batch"), axis=0)
     return (hidden, weight_grad.reshape(4, feat_here, width_here))
 
 

time: 758 us -> 786 us (1.037)
  waiting for transfers between devices: 663 us -> 686 us
  other arithmetic: 11.1 us -> 21.5 us
    all_gather x0 -> x1, waiting for transfers between devices: none -> 147 us  [on_device(): weight_grad = jnp.sum(lax.all_gather(local_grad, 'batch'), axis=0)]
    psum x1 -> x0, waiting for transfers between devices: 123 us -> none  [on_device(): weight_grad = lax.psum(local_grad, 'batch')]
    reduce_sum x0 -> x1, other arithmetic: none -> 10.8 us  [on_device(): weight_grad = jnp.sum(lax.all_gather(local_grad, 'batch'), axis=0)]
where the time goes in v1:
time: 786 us; the launch traced here: 785 us
  waiting for transfers between devices  686 us (87%)
  blocking collectives  35 us (4%)
  matrix products  25.4 us (3%)
  other arithmetic  21.5 us (3%)
  between operations  15.5 us (2%)
    reduce_scatter x1, waiting for transfers between devices, on_device(): lax.psum_scatter(lax.dot_general(row_block, weights, (((1,), (1,)), ((),...  260 us
    all_gather x1, waiting for transfers between devices, on_device(): weight_grad = jnp.sum(lax.all_gather(local_grad, 'batch'), axis=0)  147 us
    psum x1, waiting for transfers between devices, on_device(): audio_part = lax.psum(partial_audio, 'hidden')  135 us
    all_gather x1, waiting for transfers between devices, on_device(): lax.all_gather(audio_grad, 'hidden', axis=0, tiled=True)  67.6 us
    all_gather x1, waiting for transfers between devices, on_device(): lax.all_gather(normed, 'batch', axis=0, tiled=True)  48 us
    reduce_scatter x1, waiting for transfers between devices, on_device(): lax.psum_scatter(partial_pair, 'width', scatter_dimension=0, tiled=True)  28.2 us
    all_gather x1, blocking collectives, on_device(): all_pairs = lax.all_gather(grad_pair, 'width', axis=0, tiled=True)  17 us
  transfers between devices with their start and end apart: 6, of which 6 were waited for; matrix products, arithmetic and copies ran while one was open for 0% of the time, Pallas kernels for 0%

profile of v1, /device:TPU:1, one launch (start us, length us, event | category | flops | bytes accessed | tf_op | source)
XLA Modules:
  0.0 785.4 jit_solution(14353860121901255536)
XLA Ops:
  7.2 1.2 copy.10
  8.4 0.1 reshape.64
  8.5 0.4 copy-done
  9.0 2.0 fusion.8
  12.4 135.1 %all-reduce.2.cloned.1.call-done = f32[128,4096]{1,0:T(8,128)} async-done(((f32[128,4096]{1,0:T(8,128)}), f32[128,4096]{1,0:T(8,128)}) %all-reduce.2.cloned.1.call-update) | async-done | bytes 2097168 | tf_op jit(solution)/shard_map/psum | solution.py:25
  147.5 2.5 multiply_reduce_fusion
  150.0 8.9 %psum.22 = f32[128]{0:T(128)S(1)} all-reduce(f32[128]{0:T(128)S(1)} %multiply_reduce_fusion), channel_id=1, replica_groups=mesh['batch'=4,'hidden'=16,'width'=4] {'width'}, use_global_device_ids=true, to_apply=%region_2.3 | all-reduce | flops 128 | bytes 1024 | tf_op jit(solution)/shard_map/psum | solution.py:38
  158.8 3.5 multiply_convert_fusion
  162.4 48.0 %all-gather.5.cloned.1.call-done = bf16[512,4096]{1,0:T(8,128)(2,1)} async-done(((bf16[128,4096]{1,0:T(8,128)(2,1)}), bf16[512,4096]{1,0:T(8,128)(2,1)}) %all-gather.5.cloned.1.call-update) | async-done | bytes 4194320 | tf_op jit(solution)/shard_map/all_gather | solution.py:46
  210.4 9.2 %fusion.9 = f32[512,832]{0,1:T(8,128)} fusion(bf16[512,4096]{1,0:T(8,128)(2,1)} %all-gather.5.cloned.1.call-done, bf16[4096,832]{0,1:T(8,128)(2,1)} %bitcast.20), kind=kOutput, calls=%fused_computation.29 | convolution fusion | flops 3489660928 | bytes 12713984 | tf_op jit(solution)/shard_map/dot_general | solution.py:45
  219.7 28.2 %reduce-scatter.3.cloned.1.call-done = f32[128,832]{0,1:T(8,128)} async-done(((f32[512,832]{0,1:T(8,128)}), f32[128,832]{0,1:T(8,128)}) %reduce-scatter.3.cloned.1.call-update) | async-done | bytes 426000 | tf_op jit(solution)/shard_map/reduce_scatter | solution.py:50
  247.8 1.8 fusion.2
  249.7 17.0 %all_gather.16 = bf16[512,832]{0,1:T(8,128)(2,1)S(1)} all-gather(bf16[128,832]{0,1:T(8,128)(2,1)S(1)} %pad_maximum_fusion), channel_id=1, replica_groups=mesh['batch'=4,'hidden'=16,'width'=4] {'width'}, dimensions={0}, use_global_device_ids=true | all-gather | bytes 1064960 | tf_op jit(solution)/shard_map/all_gather | solution.py:65
  266.7 9.7 %fusion.10 = f32[512,4096]{1,0:T(8,128)} fusion(bf16[512,832]{0,1:T(8,128)(2,1)S(1)} %all_gather.16, bf16[4096,832]{0,1:T(8,128)(2,1)} %bitcast.21), kind=kOutput, calls=%fused_computation.30 | convolution fusion | flops 3489660928 | bytes 16056320 | tf_op jit(solution)/shard_map/dot_general | solution.py:69
  276.5 0.1 dynamic_slice.9
  276.6 260.5 %reduce-scatter.5.cloned.1.call-done = f32[8,4096]{1,0:T(8,128)} async-done(((f32[512,4096]{1,0:T(8,128)}), f32[8,4096]{1,0:T(8,128)}) %reduce-scatter.5.cloned.1.call-update) | async-done | bytes 131088 | tf_op jit(solution)/shard_map/reduce_scatter | solution.py:68
  537.0 1.1 multiply_reduce_fusion.1
  538.1 0.1 dynamic_slice.11
  538.2 9.1 %psum.23 = f32[8]{0:T(128)S(1)} all-reduce(f32[8]{0:T(128)S(1)} %multiply_reduce_fusion.1), channel_id=1, replica_groups=mesh['batch'=4,'hidden'=16,'width'=4] {'width'}, use_global_device_ids=true, to_apply=%region_6.7 | all-reduce | flops 8 | bytes 64 | tf_op jit(solution)/shard_map/psum | solution.py:81
  547.3 1.7 select_convert_fusion
  549.0 67.6 %all-gather.7.cloned.1.call-done = bf16[128,4096]{1,0:T(8,128)(2,1)} async-done(((bf16[8,4096]{1,0:T(8,128)(2,1)}), bf16[128,4096]{1,0:T(8,128)(2,1)}) %all-gather.7.cloned.1.call-update) | async-done | bytes 1048592 | tf_op jit(solution)/shard_map/all_gather | solution.py:89
  616.6 4.5 convolution_bitcast_fusion
  621.1 146.6 %all-gather.9.cloned.1.call-done = f32[1280,4096]{1,0:T(8,128)} async-done(((f32[320,4096]{1,0:T(8,128)}), f32[1280,4096]{1,0:T(8,128)}) %all-gather.9.cloned.1.call-update) | async-done | bytes 20971536 | tf_op jit(solution)/shard_map/all_gather | solution.py:93
  767.7 10.8 %reduce_sum.29 = f32[320,4096]{1,0:T(8,128)} reduce(f32[4,320,4096]{2,1,0:T(8,128)} %bitcast.19, f32[]{:T(128)} %constant.56.clone.1), dimensions={0}, to_apply=%region_7.8 | reduce | flops 3932160 | bytes 26214404 | tf_op jit(solution)/shard_map/reduce_sum | solution.py:93
  (26 shorter events, 0.4 us)
Async XLA Ops:
  7.2 1.8 copy-start
  7.2 140.3 %all-reduce.2.cloned.1.call-start = ((), (), s32[]{:S(2)}) async-start(), calls=%async_computation.2 | async-start | bytes 4194304 | tf_op jit(solution)/shard_map/psum | solution.py:25
  11.0 1.4 copy-start.4
  11.0 199.4 %all-gather.5.cloned.1.call-start = ((), (), s32[]{:S(2)}) async-start(), calls=%async_computation.3 | async-start | bytes 5242880 | tf_op jit(solution)/shard_map/all_gather | solution.py:46
  147.4 11.4 %copy-start.2 = (f32[128,4096]{1,0:T(8,128)S(1)}, f32[128,4096]{1,0:T(8,128)}, u32[]{:S(2)}) copy-start(f32[128,4096]{1,0:T(8,128)} %all-reduce.2.cloned.1.call-done) | copy-start | bytes 6291460
  162.4 85.5 %reduce-scatter.3.cloned.1.call-start = ((), (), s32[]{:S(2)}) async-start(), calls=%async_computation.4 | async-start | bytes 2129920 | tf_op jit(solution)/shard_map/reduce_scatter | solution.py:50
  210.4 37.4 %copy-start.3 = (bf16[128,416]{0,1:T(8,128)(2,1)S(1)}, bf16[128,416]{0,1:T(8,128)(2,1)}, u32[]{:S(2)}) copy-start(bf16[128,416]{0,1:T(8,128)(2,1)} %param.15) | copy-start | bytes 319492
  219.6 317.4 %reduce-scatter.5.cloned.1.call-start = ((), (), s32[]{:S(2)}) async-start(), calls=%async_computation.5 | async-start | bytes 8519680 | tf_op jit(solution)/shard_map/reduce_scatter | solution.py:68
  276.4 340.2 %all-gather.7.cloned.1.call-start = ((), (), s32[]{:S(2)}) async-start(), calls=%async_computation.6 | async-start | bytes 1114112 | tf_op jit(solution)/shard_map/all_gather | solution.py:89
  549.0 218.7 %all-gather.9.cloned.1.call-start = ((), (), s32[]{:S(2)}) async-start(), calls=%async_computation.7 | async-start | bytes 26214400 | tf_op jit(solution)/shard_map/all_gather | solution.py:93
  767.7 10.8 %copy-start.1 = (bf16[4,80,4096]{2,1,0:T(8,128)(2,1)S(1)}, bf16[4,80,4096]{2,1,0:T(8,128)(2,1)}, u32[]{:S(2)}) copy-start(bf16[4,80,4096]{2,1,0:T(8,128)(2,1)} %param.9) | copy-start | bytes 7864324
Sparse Core Ops, SparseCore 0:
  11.2 136.1 all-reduce.1
  162.5 47.8 all-gather.4
  219.7 28.0 reduce-scatter.2
  276.5 260.4 reduce-scatter.4
  549.1 67.4 all-gather.6
  621.2 146.4 all-gather.8
